TPU v7x, 32 devices: a whole 2x2x4 slice. The times are simulated.
32 devices in a mesh: seq: 8 (over z, y), head: 4 (over x, core).
Axes of the slice: x: 2, y: 2, z: 4, core: 2. Of those that a mesh axis runs over, the one named last changes fastest.
Arguments:
- hidden: bfloat16 [4096, 8192], P('seq'), may hold values from -6 to 6
- w_query: bfloat16 [8192, 4096], P('seq', 'head'), may hold values from -0.0625 to 0.0625
- w_key: bfloat16 [8192, 4096], P('seq', 'head'), may hold values from -0.0625 to 0.0625
- w_value: bfloat16 [8192, 4096], P('seq', 'head'), may hold values from -0.0625 to 0.0625
- cotangent: bfloat16 [4096, 4096], P('seq', 'head'), may hold values from -6 to 6
Outputs:
- step_direction: float32 [4096, 8192], P(('seq', 'head'))
All inputs are finite; a program needn't handle non-finite values.
Results may differ from a plain program's by a relative error of at most 0.015.
Values may be sent and summed in bfloat16 or wider, within the bound.
A program may use at most 192 MiB of HBM per device.

v0:
```python
import functools

import jax
import jax.numpy as jnp
from jax import lax
from jax.experimental import pallas as pl
from jax.experimental.pallas import tpu as pltpu
from jax.sharding import PartitionSpec as P

DH = 128
NORM_EPS = 1e-05
STEP_EPS = 1e-06


F32 = jnp.float32
BF16 = jnp.bfloat16
MESH = pl.DeviceIdType.MESH
VMEM_LIMIT = 64000 * 1024
ROW_CUTS = 2
LEAD = 2


def silu_slope(preact):
    sigmoid = jax.nn.sigmoid(preact)
    return sigmoid * (1.0 + preact * (1.0 - sigmoid))


def swap(value, axis, mask, size):
    return lax.ppermute(value, axis, [(i, i ^ mask) for i in range(size)])


def flip(index, mask):
    bit = 1
    while bit <= mask:
        if mask & bit:
            index = index + bit * (1 - 2 * ((index // bit) % 2))
        bit *= 2
    return index


def xor(left, right, size):
    total, bit = 0, 1
    while bit < size:
        total = total + bit * ((left // bit + right // bit) % 2)
        bit *= 2
    return total


def bits_below(top):
    masks, bit = [], 1
    while bit < top:
        masks.append(bit)
        bit *= 2
    return masks


def greet(partners):
    barrier = pltpu.get_barrier_semaphore()
    for where in partners:
        pl.semaphore_signal(barrier, inc=1, device_id=where, device_id_type=MESH)
    pl.semaphore_wait(barrier, len(partners))


def gather_kernel(seq_count, head_parts, hidden, w_key, w_value, w_query, cot,
                  gathered, pre, cot_other, tokens, own, stage,
                  w_send, w_recv, tok_send, tok_recv, cot_sems, local, fetch):
    seat = lax.axis_index("seq")
    lane = lax.axis_index("head")
    tok_rows, _ = hidden.shape
    row_block, col_width = w_key.shape
    half = col_width // 2
    col_piece = stage.shape[2]
    row_piece = stage.shape[1]
    top, pair = seq_count // 2, seq_count // 4
    bit = (seat // pair) % 2
    low_masks = bits_below(pair)
    far_masks = (top | pair, top, pair)
    head_masks = bits_below(head_parts)
    share = tok_rows // head_parts
    weights = (w_key, w_value, w_query)
    pieces = [
        (proj, ch, r)
        for proj in range(3)
        for ch in range(half // col_piece)
        for r in range(row_block // row_piece)
    ]

    def seq_id(mask):
        return (flip(seat, mask), lane)

    def head_id(mask):
        return (seat, flip(lane, mask))

    greet([seq_id(m) for m in far_masks] + [seq_id(m) for m in low_masks]
          + [head_id(m) for m in head_masks])

    def remote(src, dst, send, recv, where):
        return pltpu.make_async_remote_copy(
            src_ref=src, dst_ref=dst, send_sem=send, recv_sem=recv,
            device_id=where, device_id_type=MESH,
        )

    def held(mask, p):
        proj, ch, r = pieces[p]
        return gathered.at[
            mask, pl.ds(r * row_piece, row_piece), pl.ds(proj * half + ch * col_piece, col_piece)
        ]

    def first_hop(mask, p):
        proj, ch, r = pieces[p]
        side = 1 - bit if mask & pair else bit
        column = pl.multiple_of(side * half + ch * col_piece, col_piece)
        src = weights[proj].at[pl.ds(r * row_piece, row_piece), pl.ds(column, col_piece)]
        return remote(src, held(mask, p), w_send.at[mask, p], w_recv.at[mask, p], seq_id(mask))

    def later_hop(mask, low, p):
        return remote(held(mask, p), held(mask ^ low, p), w_send.at[mask ^ low, p],
                      w_recv.at[mask ^ low, p], seq_id(low))

    def tok_rows_of(index, who):
        return tokens.at[index, pl.ds(pl.multiple_of(who * share, share), share)]

    tok_in = remote(
        hidden.at[pl.ds(pl.multiple_of(lane * share, share), share)], tok_rows_of(bit, lane),
        tok_send.at[0], tok_recv.at[0], seq_id(pair),
    )
    tok_in.start()
    sends = []
    for p in range(len(pieces)):
        for mask in low_masks:
            copy = first_hop(mask, p)
            copy.start()
            sends.append(copy)
    for p in range(-LEAD, len(pieces)):
        if p + LEAD < len(pieces):
            copy = first_hop(pair, p + LEAD)
            copy.start()
            sends.append(copy)
        if p >= 0:
            for mask in (top | pair, top):
                copy = first_hop(mask, p)
                copy.start()
                sends.append(copy)
        if p == -LEAD:
            side = pl.multiple_of((1 - bit) * half, half)
            cot_copy = remote(cot.at[:, pl.ds(side, half)], cot_other,
                              cot_sems.at[0], cot_sems.at[1], seq_id(pair))
            cot_copy.start()

    own_copies = []
    for proj in range(3):
        copy = pltpu.make_async_copy(
            weights[proj].at[:, pl.ds(pl.multiple_of(bit * half, half), half)],
            own.at[:, pl.ds(proj * half, half)], local.at[proj])
        copy.start()
        own_copies.append(copy)
    tok_local = pltpu.make_async_copy(hidden, tokens.at[bit], local.at[3])
    tok_local.start()
    for copy in own_copies:
        copy.wait()
    own_out = pltpu.make_async_copy(own, gathered.at[0], local.at[4])
    own_out.start()
    own_out.wait()
    tok_local.wait()

    def wait_recv(mask, p):
        here = held(mask, p)
        remote(here, here, w_send.at[mask, p], w_recv.at[mask, p], seq_id(pair)).wait_recv()

    arrived = set()

    def ensure(mask, p):
        if (mask, p) not in arrived:
            arrived.add((mask, p))
            wait_recv(mask, p)

    def spread(base, p):
        for low in low_masks:
            for sub in range(low):
                if base | sub:
                    ensure(base | sub, p)
                    copy = later_hop(base | sub, low, p)
                    copy.start()
                    sends.append(copy)

    def passes(p):
        for q in range(LEAD) if p == 0 else ():
            spread(pair, q)
        if p + LEAD < len(pieces):
            spread(pair, p + LEAD)
        spread(top | pair, p)
        spread(top, p)
        spread(0, p)

    def token_hop(step, mask, carried):
        copies = []
        for k, sub in enumerate(carried):
            block = tok_rows_of(1 - bit, flip(lane, sub))
            copy = remote(block, block, tok_send.at[step + k], tok_recv.at[step + k],
                          head_id(mask))
            copy.start()
            copies.append(copy)
        return copies

    hops = list(reversed(head_masks))
    carried = [0]

    def project(p):
        proj, ch, r = pieces[p]
        for mask in range(1, seq_count):
            ensure(mask, p)
        copies = []
        for mask in range(seq_count):
            copy = pltpu.make_async_copy(held(mask, p), stage.at[mask], fetch.at[mask])
            copy.start()
            copies.append(copy)
        for copy in copies:
            copy.wait()
        columns = pl.ds(ch * col_piece, col_piece)

        def block_dot(mask, carry):
            block = xor(seat, mask, seq_count)
            offset = pl.multiple_of(block * row_block + r * row_piece, row_piece)
            for side in range(2):
                term = jnp.dot(tokens[side, :, pl.ds(offset, row_piece)], stage[mask],
                               preferred_element_type=F32)
                pre[proj, side, :, columns] += term
            return carry

        if r == 0:
            for side in range(2):
                pre[proj, side, :, columns] = jnp.zeros((tok_rows, col_piece), F32)
        lax.fori_loop(0, seq_count, block_dot, 0)

    tok_copies = [tok_in]
    hops = list(reversed(head_masks))

    carried, flight, hop = [0], [tok_in], 0
    pending = []
    for p in range(len(pieces)):
        passes(p)
        pending.append(p)
        while hop <= len(hops) and (p >= 2 * hop + 1 or p == len(pieces) - 1):
            for copy in flight:
                copy.wait_recv()
            if hop < len(hops):
                flight = token_hop(len(tok_copies), hops[hop], carried)
                tok_copies += flight
                carried = carried + [c ^ hops[hop] for c in carried]
            hop += 1
        if hop > len(hops):
            for q in pending:
                project(q)
            pending = []
    for copy in sends:
        copy.wait_send()
    for copy in tok_copies:
        copy.wait_send()
    cot_copy.wait()


def gather_project(seq_count, head_parts, hidden, w_query, w_key, w_value, cotangent):
    tok_rows, width = hidden.shape
    row_block, col_width = w_query.shape
    half = col_width // 2
    col_piece = min(half, 256)
    row_piece = row_block // ROW_CUTS
    n_pieces = 3 * (half // col_piece) * ROW_CUTS
    anyspace = pl.BlockSpec(memory_space=pl.ANY)
    return pl.pallas_call(
        functools.partial(gather_kernel, seq_count, head_parts),
        name="gather_project",
        out_shape=(
            jax.ShapeDtypeStruct((seq_count, row_block, 3 * half), BF16),
            jax.ShapeDtypeStruct((3, 2, tok_rows, half), F32),
            jax.ShapeDtypeStruct((tok_rows, half), BF16),
        ),
        in_specs=[anyspace] * 5,
        out_specs=(anyspace, pl.BlockSpec(memory_space=pltpu.VMEM), anyspace),
        scratch_shapes=[
            pltpu.VMEM((2, tok_rows, width), BF16),
            pltpu.VMEM((row_block, 3 * half), BF16),
            pltpu.VMEM((seq_count, row_piece, col_piece), BF16),
            pltpu.SemaphoreType.DMA((seq_count, n_pieces)),
            pltpu.SemaphoreType.DMA((seq_count, n_pieces)),
            pltpu.SemaphoreType.DMA((head_parts,)),
            pltpu.SemaphoreType.DMA((head_parts,)),
            pltpu.SemaphoreType.DMA((2,)),
            pltpu.SemaphoreType.DMA((5,)),
            pltpu.SemaphoreType.DMA((seq_count,)),
        ],
        compiler_params=pltpu.CompilerParams(
            collective_id=0, has_side_effects=True, vmem_limit_bytes=VMEM_LIMIT
        ),
    )(hidden, w_key, w_value, w_query, cotangent)


def reduce_kernel(seq_count, head_parts, kt, lag, back, gathered, out, *scratch):
    seat = lax.axis_index("seq")
    lane = lax.axis_index("head")
    out_rows = back.shape[1]
    row_block, _ = gathered.shape[1:]
    per_block = row_block // kt
    n_tiles = seq_count * per_block
    pair = seq_count // 4
    bit = (seat // pair) % 2
    head_masks = bits_below(head_parts)
    nd = len(head_masks) + 1
    groups = 2 ** nd
    dims = [((seat, flip(lane, m)), nd - 1 - k) for k, m in enumerate(head_masks)]
    dims.append(((flip(seat, pair), lane), 0))
    orders = (
        list(range(nd)),
        [0, nd - 1] + list(range(1, nd - 1)),
    )
    rel, w_slots = scratch[0], scratch[1]
    keeps = scratch[2:2 + nd]
    send_bufs = scratch[2 + nd:2 + 2 * nd]
    recv_bufs = scratch[2 + 2 * nd:2 + 3 * nd]
    w_sem, send_sem, recv_sem = scratch[2 + 3 * nd:]

    greet([where for where, _ in dims])

    base = seat - bit * pair

    def fetch(j):
        block = xor(j // per_block, bit * pair, seq_count)
        row = pl.multiple_of((j % per_block) * kt, kt)
        return pltpu.make_async_copy(
            gathered.at[block, pl.ds(row, kt)], w_slots.at[j % 2], w_sem.at[j % 2])

    fetch(0).start()
    for g in range(groups):
        far_side = g % 2
        who = lane
        for k, m in enumerate(head_masks):
            if (g >> (nd - 1 - k)) & 1:
                who = flip(who, m)
        side = flip(bit, 1) if far_side else bit
        rel[pl.ds(g * out_rows, out_rows)] = back[side * head_parts + who]

    plans = []
    for order in orders:
        plan, current = [], list(range(groups))
        for d in order:
            place = dims[d][1]
            sent = [i for i, g in enumerate(current) if (g >> place) & 1]
            kept = [i for i, g in enumerate(current) if not (g >> place) & 1]
            plan.append((d, sent, kept))
            current = [current[i] for i in kept]
        plans.append(plan)

    def copy_of(stage, tile, where):
        return pltpu.make_async_remote_copy(
            src_ref=send_bufs[stage].at[tile], dst_ref=recv_bufs[stage].at[tile],
            send_sem=send_sem.at[stage, tile], recv_sem=recv_sem.at[stage, tile],
            device_id=where, device_id_type=MESH)

    rows_half = groups // 2 * out_rows

    def multiply(j, plan):
        fetch(j).wait()

        @pl.when(j + 1 < n_tiles)
        def _():
            fetch(j + 1).start()

        w = w_slots[j % 2]
        contract = (((1,), (1,)), ((), ()))
        away = lax.dot_general(rel[pl.ds(rows_half, rows_half)], w, contract,
                               preferred_element_type=F32)
        send_bufs[0][j] = away.astype(BF16).reshape(groups // 2, out_rows, kt)
        copy_of(0, j, dims[plan[0][0]][0]).start()
        home = lax.dot_general(rel[pl.ds(0, rows_half)], w, contract, preferred_element_type=F32)
        keeps[0][j % keeps[0].shape[0]] = home.reshape(groups // 2, out_rows, kt)

    def forward(stage, j, plan):
        copy_of(stage - 1, j, dims[plan[stage - 1][0]][0]).wait_recv()
        slot = j % keeps[stage - 1].shape[0]
        if stage == nd:
            total = keeps[stage - 1][slot, 0] + recv_bufs[stage - 1][j, 0].astype(F32)
            block = xor(base, j // per_block, seq_count)
            column = pl.multiple_of(block * row_block + (j % per_block) * kt, kt)
            out[:, pl.ds(column, kt)] = total
            return
        d, sent, kept = plan[stage]
        for k, i in enumerate(sent):
            total = keeps[stage - 1][slot, i] + recv_bufs[stage - 1][j, i].astype(F32)
            send_bufs[stage][j, k] = total.astype(BF16)
        copy_of(stage, j, dims[d][0]).start()
        here = j % keeps[stage].shape[0]
        for k, i in enumerate(kept):
            keeps[stage][here, k] = keeps[stage - 1][slot, i] + recv_bufs[stage - 1][j, i].astype(F32)

    delays = [0] + [1 + lag * s for s in range(nd)]
    steps = n_tiles + delays[-1]

    def step(i, carry):
        for parity in range(2):
            now = i * 2 + parity

            @pl.when(now < n_tiles)
            def _():
                multiply(now, plans[parity])

            for stage in range(1, nd + 1):
                j = now - delays[stage]
                plan = plans[(parity - delays[stage]) % 2]

                @pl.when((j >= 0) & (j < n_tiles))
                def _():
                    forward(stage, j, plan)
        return carry

    lax.fori_loop(0, (steps + 1) // 2, step, 0)

    def drain(j, carry):
        for stage in range(nd):
            copy_of(stage, j, dims[0][0]).wait_send()
        return carry

    lax.fori_loop(0, n_tiles, drain, 0)


def project_back(seq_count, head_parts, back, gathered):
    groups, out_rows, depth = back.shape
    row_block = gathered.shape[1]
    kt = row_block // 2
    n_tiles = seq_count * 2
    lag = 3
    nd = len(bits_below(head_parts)) + 1
    sizes = [groups >> (s + 1) for s in range(nd)]
    return pl.pallas_call(
        functools.partial(reduce_kernel, seq_count, head_parts, kt, lag),
        name="project_back",
        out_shape=jax.ShapeDtypeStruct((out_rows, seq_count * row_block), F32),
        in_specs=[pl.BlockSpec(memory_space=pltpu.VMEM), pl.BlockSpec(memory_space=pl.ANY)],
        out_specs=pl.BlockSpec(memory_space=pltpu.VMEM),
        scratch_shapes=[
            pltpu.VMEM((groups * out_rows, depth), BF16),
            pltpu.VMEM((2, kt, depth), BF16),
            *[pltpu.VMEM((2 if s == 0 else lag + 1, n, out_rows, kt), F32)
              for s, n in enumerate(sizes)],
            *[pltpu.VMEM((n_tiles, n, out_rows, kt), BF16) for n in sizes],
            *[pltpu.VMEM((n_tiles, n, out_rows, kt), BF16) for n in sizes],
            pltpu.SemaphoreType.DMA((2,)),
            pltpu.SemaphoreType.DMA((nd, n_tiles)),
            pltpu.SemaphoreType.DMA((nd, n_tiles)),
        ],
        compiler_params=pltpu.CompilerParams(
            collective_id=1, has_side_effects=True, vmem_limit_bytes=VMEM_LIMIT
        ),
    )(back, gathered)


def scan_states(own, seq_count, later):
    seat = lax.axis_index("seq")
    top, pair = seq_count // 2, seq_count // 4
    total = own
    outside = jnp.zeros_like(own)
    for mask in bits_below(pair):
        other = swap(total.astype(BF16), "seq", mask, seq_count).astype(F32)
        wanted = (seat & mask) == (0 if later else mask)
        outside = outside + jnp.where(wanted, other, 0.0)
        total = total + other
    if later:
        outside = outside.at[0].add(total[1])
    else:
        outside = outside.at[1].add(total[0])
    whole = total[0] + total[1]
    other = swap(whole.astype(BF16), "seq", top, seq_count).astype(F32)
    wanted = (seat & top) == (0 if later else top)
    return outside + jnp.where(wanted, other, 0.0)[None]


def attend(seq_count, pre, cot):
    _, _, tok_rows, cols = pre.shape
    shape = (2, tok_rows, cols // DH, DH)
    pre_key, pre_value, pre_query = (pre[i].reshape(shape) for i in range(3))
    key_rows = jax.nn.silu(pre_key).astype(BF16)
    value_rows = pre_value.astype(BF16)
    query_rows = jax.nn.silu(pre_query).astype(BF16)
    own_state = jnp.einsum("bthi,bthj->bhij", key_rows, value_rows, preferred_element_type=F32)
    before = scan_states(own_state, seq_count, False)
    causal = (
        lax.broadcasted_iota(jnp.int32, (tok_rows, tok_rows), 0)
        >= lax.broadcasted_iota(jnp.int32, (tok_rows, tok_rows), 1)
    )[None, None]
    scores = jnp.einsum("bthd,bshd->bhts", query_rows, key_rows, preferred_element_type=F32)
    score_rows = jnp.where(causal, scores, 0.0).astype(BF16)
    inside = jnp.einsum("bhts,bshd->bthd", score_rows, value_rows, preferred_element_type=F32)
    carried = jnp.einsum(
        "bthi,bhij->bthj", query_rows.astype(F32), before, precision=lax.Precision.HIGHEST
    )
    attended = inside + carried
    scale = lax.rsqrt(jnp.mean(attended * attended, axis=-1, keepdims=True) + NORM_EPS)
    normed = attended * scale
    upstream = cot.astype(F32).reshape(shape)
    grad_att = (
        scale * (upstream - normed * jnp.mean(upstream * normed, axis=-1, keepdims=True))
    ).astype(BF16)
    own_grad = jnp.einsum("bthi,bthj->bhij", query_rows, grad_att, preferred_element_type=F32)
    later_sum = scan_states(own_grad, seq_count, True)
    grad_scores = jnp.einsum("bthd,bshd->bhts", grad_att, value_rows, preferred_element_type=F32)
    grad_scores = jnp.where(causal, grad_scores, 0.0).astype(BF16)
    highest = lax.Precision.HIGHEST
    grad_query = jnp.einsum(
        "bhts,bshd->bthd", grad_scores, key_rows, preferred_element_type=F32
    ) + jnp.einsum("bthj,bhij->bthi", grad_att.astype(F32), before, precision=highest)
    grad_key = jnp.einsum(
        "bhts,bthd->bshd", grad_scores, query_rows, preferred_element_type=F32
    ) + jnp.einsum("bthj,bhij->bthi", value_rows.astype(F32), later_sum, precision=highest)
    grad_value = jnp.einsum(
        "bhts,bthd->bshd", score_rows, grad_att, preferred_element_type=F32
    ) + jnp.einsum("bthi,bhij->bthj", key_rows.astype(F32), later_sum, precision=highest)
    back_key = (grad_key * silu_slope(pre_key)).astype(BF16)
    back_value = grad_value.astype(BF16)
    back_query = (grad_query * silu_slope(pre_query)).astype(BF16)
    return jnp.concatenate(
        [b.reshape(2, tok_rows, cols) for b in (back_key, back_value, back_query)], axis=2
    )


def on_device(seq_count, head_parts, hidden, w_query, w_key, w_value, cotangent):
    tok_rows, _ = hidden.shape
    half = w_query.shape[1] // 2
    seat = lax.axis_index("seq")
    bit = (seat // (seq_count // 4)) % 2
    gathered, pre, cot_other = gather_project(
        seq_count, head_parts, hidden, w_query, w_key, w_value, cotangent
    )
    cot_own = lax.dynamic_slice_in_dim(cotangent, bit * half, half, 1)
    cot = jnp.where(
        bit == 0, jnp.stack([cot_own, cot_other]), jnp.stack([cot_other, cot_own])
    )
    back = attend(seq_count, pre, cot)
    back = back.reshape(2 * head_parts, tok_rows // head_parts, 3 * half)
    input_grad = project_back(seq_count, head_parts, back, gathered)
    factor = lax.rsqrt(jnp.mean(input_grad * input_grad, axis=-1, keepdims=True) + STEP_EPS)
    return jnp.tanh(input_grad * factor)


def solution(mesh):
    def body(*args):
        return on_device(mesh.shape["seq"], mesh.shape["head"], *args)

    return jax.shard_map(
        body,
        mesh=mesh,
        in_specs=(
            P("seq", None),
            P("seq", "head"),
            P("seq", "head"),
            P("seq", "head"),
            P("seq", "head"),
        ),
        out_specs=P(("seq", "head"), None),
        check_vma=False,
    )
```

profile of v0, /device:TPU:0, one launch (start us, length us, event | category | flops | bytes accessed | tf_op | source)
XLA Modules:
  0.0 531.1 jit_solution(4046126761813524493)
XLA Ops:
  0.0 361.1 %gather_project.1 = (bf16[8,1024,1536]{2,1,0:T(8,128)(2,1)}, f32[3,2,512,512]{3,2,1,0:T(8,128)}, bf16[512,512]{1,0:T(8,128)(2,1)}) custom-call(bf16[512,8192]{1,0:T(8,128)(2,1)} %hidden.1, bf16[1024,1024]{1,0:T(8,128)(2,1)} %w_key.1, bf16[1024,1024]{1,0:T(8,128)(2,1)} %w_value.1, bf16[1024,1024]{1,0:T(8,128)(2,1)} %w_query.1, bf16[512,1024]{1,0:T(8,128)(2,1)} %cot.1), custom_call_target="tpu_custom_call" | custom-call | tf_op jit(solution)/shard_map/gather_project/pallas_call | solution.py:270
  361.1 2.7 slice.119
  363.8 4.2 fusion.27
  369.4 2.9 copy.41
  372.3 1.8 copy.40
  374.2 3.3 multiply_convert_fusion
  379.0 1.4 select_convert_fusion.1
  380.4 5.1 collective-permute-done
  385.5 1.9 convert_add_fusion.1
  387.4 1.7 fusion.25
  389.1 2.9 fusion.7
  392.0 1.9 constant_dynamic-slice_fusion
  393.8 2.0 copy.16
  395.9 2.1 copy.42
  398.9 3.1 fusion.5
  403.4 1.5 select_convert_fusion
  405.1 1.5 fusion.32
  406.6 3.9 fusion.3
  410.4 2.1 fusion.31
  413.4 1.7 fusion.26
  415.1 2.9 collective-permute-start.3
  418.0 2.3 fusion.30
  420.3 1.7 copy.30
  423.3 3.8 fusion.6
  427.1 2.5 copy.27
  429.7 2.2 concatenate.17
  431.9 4.3 fusion.4
  436.2 1.8 copy.24
  439.3 2.8 pad_maximum_fusion.back
  442.2 82.8 %project_back.1 = f32[128,8192]{1,0:T(8,128)} custom-call(bf16[8,128,1536]{2,1,0:T(8,128)(2,1)} %pad_maximum_fusion.back, bf16[8,1024,1536]{2,1,0:T(8,128)(2,1)} %get-tuple-element.34.gathered), custom_call_target="tpu_custom_call" | custom-call | tf_op jit(solution)/shard_map/project_back/pallas_call | solution.py:433
  525.0 2.7 multiply_reduce_fusion
  528.5 2.6 multiply_tanh_fusion
  (40 shorter events, 9.6 us)
Async XLA Ops:
  378.8 6.7 %collective-permute-start = (bf16[2,4,128,128]{3,2,1,0:T(8,128)(2,1)}, bf16[2,4,128,128]{3,2,1,0:T(8,128)(2,1)}, u32[]{:S(2)}, u32[]{:S(2)}) collective-permute-start(bf16[2,4,128,128]{3,2,1,0:T(8,128)(2,1)} %get-tuple-element.45), channel_id=1, source_target_pairs={{0,4},{4,0},{8,12},{12,8},{16,20},{20,16},{24,28},{28,24},{1,5},{5... | collective-permute-start | bytes 786440 | tf_op jit(solution)/shard_map/ppermute | solution.py:29
  379.0 6.5 %copy-start.9 = (f32[2,4,128,128]{3,2,1,0:T(8,128)S(1)}, f32[2,4,128,128]{3,2,1,0:T(8,128)}, u32[]{:S(2)}) copy-start(f32[2,4,128,128]{3,2,1,0:T(8,128)} %get-tuple-element.46) | copy-start | bytes 1572868
  380.4 8.7 %copy-start.1 = (bf16[2,4,512,512]{3,2,1,0:T(8,128)(2,1)}, bf16[2,4,512,512]{3,2,1,0:T(8,128)(2,1)S(1)}, u32[]{:S(2)}) copy-start(bf16[2,4,512,512]{3,2,1,0:T(8,128)(2,1)S(1)} %select_convert_fusion.1) | copy-start | bytes 12582916
  389.1 8.9 %collective-permute-start.1 = (bf16[4,128,128]{2,1,0:T(8,128)(2,1)S(1)}, bf16[4,128,128]{2,1,0:T(8,128)(2,1)}, u32[]{:S(2)}, u32[]{:S(2)}) collective-permute-start(bf16[4,128,128]{2,1,0:T(8,128)(2,1)S(1)} %get-tuple-element.39), channel_id=1, source_target_pairs={{0,16},{4,20},{8,24},{12,28},{16,0},{20,4},{24,8},{28,12},{1,17},{... | collective-permute-start | bytes 393224 | tf_op jit(solution)/shard_map/ppermute | solution.py:29
  398.9 3.1 copy-start.5
  398.9 3.1 copy-start.6
  404.9 1.6 copy-start.4
  404.9 7.6 %collective-permute-start.2 = (bf16[2,4,128,128]{3,2,1,0:T(8,128)(2,1)S(1)}, bf16[2,4,128,128]{3,2,1,0:T(8,128)(2,1)S(1)}, u32[]{:S(2)}, u32[]{:S(2)}) collective-permute-start(bf16[2,4,128,128]{3,2,1,0:T(8,128)(2,1)S(1)} %get-tuple-element.49), channel_id=1, source_target_pairs={{0,4},{4,0},{8,12},{12,8},{16,20},{20,16},{24,28},{28,24},{1,5},{5... | collective-permute-start | bytes 786440 | tf_op jit(solution)/shard_map/ppermute | solution.py:29
  406.6 3.9 copy-start.2
  415.1 8.2 %collective-permute-start.3 = (bf16[4,128,128]{2,1,0:T(8,128)(2,1)S(1)}, bf16[4,128,128]{2,1,0:T(8,128)(2,1)S(1)}, u32[]{:S(2)}, u32[]{:S(2)}) collective-permute-start(bf16[4,128,128]{2,1,0:T(8,128)(2,1)S(1)} %get-tuple-element.37), channel_id=1, source_target_pairs={{0,16},{4,20},{8,24},{12,28},{16,0},{20,4},{24,8},{28,12},{1,17},{... | collective-permute-start | bytes 393224 | tf_op jit(solution)/shard_map/ppermute | solution.py:29
  427.1 4.8 copy-start.3
  436.2 3.1 copy-start.7
  436.2 3.1 copy-start.8
  525.0 3.5 copy-start
where the time goes:
time: 532 us; the launch traced here: 531 us
  Pallas kernels  444 us (83%)
  local copies, waits for them, and re-layouts  30.7 us (6%)
  matrix products  28.4 us (5%)
  other arithmetic  19.6 us (4%)
    pallas_call x1, Pallas kernels, gather_project(): pl.pallas_call(functools.partial(gather_kernel, seq_count, head_parts), n...  361 us
    pallas_call x1, Pallas kernels, project_back(): pl.pallas_call(functools.partial(reduce_kernel, seq_count, head_parts, kt...  82.8 us
  transfers between devices with their start and end apart: 4, of which 1 were waited for; matrix products, arithmetic and copies ran while one was open for 4% of the time, Pallas kernels for 0%

commit v1 on v0

v1 whole, which is shorter than its diff:
```python
import functools

import jax
import jax.numpy as jnp
from jax import lax
from jax.experimental import pallas as pl
from jax.experimental.pallas import tpu as pltpu
from jax.sharding import PartitionSpec as P

DH = 128
NORM_EPS = 1e-05
STEP_EPS = 1e-06


F32 = jnp.float32
BF16 = jnp.bfloat16
MESH = pl.DeviceIdType.MESH
VMEM_LIMIT = 64000 * 1024
ROW_CUTS = 2
LAST_CUTS = (2, 1, 1)
AHEAD = 2
HELD_BACK = (2, 2)
TOP_GAP = 4
TOKEN_CUTS = 4
CATCH_UP = 4


def silu_slope(preact):
    sigmoid = jax.nn.sigmoid(preact)
    return sigmoid * (1.0 + preact * (1.0 - sigmoid))


def flip(index, mask):
    bit = 1
    while bit <= mask:
        if mask & bit:
            index = index + bit * (1 - 2 * ((index // bit) % 2))
        bit *= 2
    return index


def xor(left, right, size):
    total, bit = 0, 1
    while bit < size:
        total = total + bit * ((left // bit + right // bit) % 2)
        bit *= 2
    return total


def bits_below(top):
    masks, bit = [], 1
    while bit < top:
        masks.append(bit)
        bit *= 2
    return masks


def cut_pieces(row_block, n_chunks):
    pieces = []
    for ch in range(n_chunks):
        for proj in range(3):
            last = ch == n_chunks - 1 and proj == 2
            row = 0
            for share in LAST_CUTS if last else (2,) * ROW_CUTS:
                rows = row_block // ROW_CUTS // 2 * share
                pieces.append((proj, ch, row, rows))
                row += rows
    return pieces


def greet(partners):
    barrier = pltpu.get_barrier_semaphore()
    for where in partners:
        pl.semaphore_signal(barrier, inc=1, device_id=where, device_id_type=MESH)
    pl.semaphore_wait(barrier, len(partners))


def layer_kernel(seq_count, head_parts, hidden, w_key, w_value, w_query, cot,
                 gathered, back, tokens, own, stage, pre, act, scores, grads, cot_rows,
                 outside, total, low_send, low_recv, top_send, top_recv,
                 w_send, w_recv, tok_send, tok_recv, cot_sems, local, fetch,
                 low_sems, top_sems):
    seat = lax.axis_index("seq")
    lane = lax.axis_index("head")
    tok_rows, _ = hidden.shape
    row_block, col_width = w_key.shape
    half = col_width // 2
    _, col_piece = stage.shape[1:]
    top, pair = seq_count // 2, seq_count // 4
    bit = (seat // pair) % 2
    low_masks = bits_below(pair)
    far_masks = (top | pair, top, pair)
    head_masks = bits_below(head_parts)
    share = tok_rows // head_parts
    weights = (w_key, w_value, w_query)
    n_chunks = half // col_piece
    chunk_heads = col_piece // DH
    pieces = cut_pieces(row_block, n_chunks)

    def seq_id(mask):
        return (flip(seat, mask), lane)

    def head_id(mask):
        return (seat, flip(lane, mask))

    greet([seq_id(m) for m in far_masks] + [seq_id(m) for m in low_masks]
          + [head_id(m) for m in head_masks])

    def remote(src, dst, send, recv, where):
        return pltpu.make_async_remote_copy(
            src_ref=src, dst_ref=dst, send_sem=send, recv_sem=recv,
            device_id=where, device_id_type=MESH,
        )

    sends = []

    def start(copy):
        copy.start()
        sends.append(copy)
        return copy


    def held(mask, p):
        proj, ch, row, rows = pieces[p]
        return gathered.at[
            mask, pl.ds(row, rows), pl.ds(proj * half + ch * col_piece, col_piece)
        ]

    def first_hop(mask, p):
        proj, ch, row, rows = pieces[p]
        side = 1 - bit if mask & pair else bit
        column = pl.multiple_of(side * half + ch * col_piece, col_piece)
        src = weights[proj].at[pl.ds(row, rows), pl.ds(column, col_piece)]
        return remote(src, held(mask, p), w_send.at[mask, p], w_recv.at[mask, p], seq_id(mask))

    def later_hop(mask, low, p):
        return remote(held(mask, p), held(mask | low, p), w_send.at[mask | low, p],
                      w_recv.at[mask | low, p], seq_id(low))

    arrived = set()

    def ensure(mask, p):
        if (mask, p) not in arrived:
            arrived.add((mask, p))
            here = held(mask, p)
            remote(here, here, w_send.at[mask, p], w_recv.at[mask, p], seq_id(pair)).wait_recv()

    def spread(base, p):
        for low in low_masks:
            for sub in range(low):
                if base | sub:
                    ensure(base | sub, p)
                    start(later_hop(base | sub, low, p))


    slab = share // TOKEN_CUTS
    hops = list(reversed(head_masks))

    def tok_block(index, who, cut):
        row = pl.multiple_of(who * share + cut * slab, slab)
        return tokens.at[index, pl.ds(row, slab)]

    def token_first(cut):
        row = pl.multiple_of(lane * share + cut * slab, slab)
        return remote(hidden.at[pl.ds(row, slab)], tok_block(bit, lane, cut),
                      tok_send.at[cut, 0], tok_recv.at[cut, 0], seq_id(pair))

    flights = {}

    def token_hop(cut, hop):
        for copy in flights[cut]:
            copy.wait_recv()
        if hop < len(hops):
            count = 2 ** hop
            held_shares = [0]
            for mask in hops[:hop]:
                held_shares = held_shares + [c ^ mask for c in held_shares]
            flights[cut] = []
            for k, sub in enumerate(held_shares):
                block = tok_block(1 - bit, flip(lane, sub), cut)
                flights[cut].append(start(remote(
                    block, block, tok_send.at[cut, count + k], tok_recv.at[cut, count + k],
                    head_id(hops[hop]))))

    side = pl.multiple_of((1 - bit) * half, half)
    cot_copy = remote(cot.at[:, pl.ds(side, half)], cot_rows.at[bit],
                      cot_sems.at[0], cot_sems.at[1], seq_id(pair))

    def issue(p):
        for mask in (top | pair, top, pair):
            start(first_hop(mask, p))
        for mask in low_masks:
            start(first_hop(mask, p))
        for cut in range(TOKEN_CUTS):
            if cut // 2 == p:
                flights[cut] = [start(token_first(cut))]
        if p == TOKEN_CUTS:
            start(cot_copy)

    issued = [0]

    def issue_to(count):
        while issued[0] < min(count, len(pieces)):
            issue(issued[0])
            issued[0] += 1

    issue_to(len(pieces) - HELD_BACK[0] if n_chunks > 1 else len(pieces))

    mine = pl.multiple_of(bit * half, half)
    own_copies = []
    for proj in range(3):
        copy = pltpu.make_async_copy(weights[proj].at[:, pl.ds(mine, half)],
                                     own.at[:, pl.ds(proj * half, half)], local.at[proj])
        copy.start()
        own_copies.append(copy)
    tok_local = pltpu.make_async_copy(hidden, tokens.at[bit], local.at[3])
    tok_local.start()
    cot_local = pltpu.make_async_copy(cot.at[:, pl.ds(mine, half)], cot_rows.at[bit], local.at[5])
    for copy in own_copies:
        copy.wait()
    own_out = pltpu.make_async_copy(own, gathered.at[0], local.at[4])
    own_out.start()
    own_out.wait()
    tok_local.wait()

    def project(p):
        proj, ch, row, rows = pieces[p]
        for mask in range(1, seq_count):
            ensure(mask, p)
        copies = []
        for mask in range(seq_count):
            copy = pltpu.make_async_copy(
                held(mask, p), stage.at[mask, pl.ds(0, rows)], fetch.at[mask])
            copy.start()
            copies.append(copy)
        for copy in copies:
            copy.wait()
        columns = pl.ds(ch * col_piece, col_piece)

        def block_dot(mask, carry):
            block = xor(seat, mask, seq_count)
            offset = pl.multiple_of(block * row_block + row, DH)
            for side in range(2):
                term = jnp.dot(tokens[side, :, pl.ds(offset, rows)], stage[mask, pl.ds(0, rows)],
                               preferred_element_type=F32)
                pre[proj, side, :, columns] += term
            return carry

        if row == 0:
            for side in range(2):
                pre[proj, side, :, columns] = jnp.zeros((tok_rows, col_piece), F32)
        lax.fori_loop(0, seq_count, block_dot, 0)


    def per_item(ch, work):
        def item(i, carry):
            head = ch * chunk_heads + i % chunk_heads
            work(i // chunk_heads, head, pl.ds(pl.multiple_of(head * DH, DH), DH))
            return carry

        lax.fori_loop(0, 2 * chunk_heads, item, 0)

    causal = (
        lax.broadcasted_iota(jnp.int32, (tok_rows, tok_rows), 0)
        >= lax.broadcasted_iota(jnp.int32, (tok_rows, tok_rows), 1)
    )

    def dot(left, right, left_dim, right_dim):
        return lax.dot_general(left, right, (((left_dim,), (right_dim,)), ((), ())),
                               preferred_element_type=F32)

    def states(side, head, cols):
        key = jax.nn.silu(pre[0, side, :, cols]).astype(BF16)
        value = pre[1, side, :, cols].astype(BF16)
        act[0, side, :, cols] = key
        act[1, side, :, cols] = value
        total[0, side, head] = dot(key, value, 0, 0)
        outside[0, side, head] = jnp.zeros((DH, DH), F32)

    def forward(side, head, cols):
        query = jax.nn.silu(pre[2, side, :, cols]).astype(BF16)
        act[2, side, :, cols] = query
        key, value = act[0, side, :, cols], act[1, side, :, cols]
        masked = jnp.where(causal, dot(query, key, 1, 1), 0.0).astype(BF16)
        scores[side, head] = masked
        attended = dot(masked, value, 1, 0) + dot(query, outside[0, side, head].astype(BF16), 1, 0)
        scale = lax.rsqrt(jnp.mean(attended * attended, axis=-1, keepdims=True) + NORM_EPS)
        normed = attended * scale
        upstream = cot_rows[side, :, cols].astype(F32)
        grad = scale * (upstream - normed * jnp.mean(upstream * normed, axis=-1, keepdims=True))
        grad = grad.astype(BF16)
        grads[side, :, cols] = grad
        total[1, side, head] = dot(query, grad, 0, 0)
        outside[1, side, head] = jnp.zeros((DH, DH), F32)

    def backward(side, head, cols):
        key, value, query = (act[i, side, :, cols] for i in range(3))
        grad = grads[side, :, cols]
        before = outside[0, side, head].astype(BF16)
        after = outside[1, side, head].astype(BF16)
        grad_scores = jnp.where(causal, dot(grad, value, 1, 1), 0.0).astype(BF16)
        grad_query = dot(grad_scores, key, 1, 0) + dot(grad, before, 1, 1)
        grad_key = dot(grad_scores, query, 0, 0) + dot(value, after, 1, 1)
        grad_value = dot(scores[side, head], grad, 0, 0) + dot(key, after, 1, 0)
        results = (
            grad_key * silu_slope(pre[0, side, :, cols]),
            grad_value,
            grad_query * silu_slope(pre[2, side, :, cols]),
        )
        for proj, result in enumerate(results):
            column = pl.ds(pl.multiple_of(proj * half + head * DH, DH), DH)
            back[side, :, column] = result.astype(BF16)


    def heads_of(ch):
        return range(ch * chunk_heads, (ch + 1) * chunk_heads)

    def low_copy(kind, ch, i):
        return remote(low_send.at[kind, ch, i], low_recv.at[kind, ch, i],
                      low_sems.at[0, kind, ch, i], low_sems.at[1, kind, ch, i],
                      seq_id(low_masks[i]))

    def top_copy(kind, ch):
        return remote(top_send.at[kind, ch], top_recv.at[kind, ch],
                      top_sems.at[0, kind, ch], top_sems.at[1, kind, ch], seq_id(top))

    def scan_send(kind, ch, i):
        for side in range(2):
            for k, head in enumerate(heads_of(ch)):
                low_send[kind, ch, i, side, k] = total[kind, side, head].astype(BF16)
        start(low_copy(kind, ch, i))

    def scan_low(kind, ch):
        for i, low in enumerate(low_masks):
            low_copy(kind, ch, i).wait_recv()
            wanted = (seat // low) % 2 == 1 - kind
            for side in range(2):
                for k, head in enumerate(heads_of(ch)):
                    other = low_recv[kind, ch, i, side, k].astype(F32)
                    outside[kind, side, head] += jnp.where(wanted, other, 0.0)
                    total[kind, side, head] += other
            if i + 1 < len(low_masks):
                scan_send(kind, ch, i + 1)
        for k, head in enumerate(heads_of(ch)):
            outside[kind, 1 - kind, head] += total[kind, kind, head]
            whole = total[kind, 0, head] + total[kind, 1, head]
            top_send[kind, ch, k] = whole.astype(BF16)
        start(top_copy(kind, ch))

    def scan_top(kind, ch):
        top_copy(kind, ch).wait_recv()
        wanted = (seat // top) % 2 == 1 - kind
        for k, head in enumerate(heads_of(ch)):
            other = jnp.where(wanted, top_recv[kind, ch, k].astype(F32), 0.0)
            for side in range(2):
                outside[kind, side, head] += other

    def stage_states(ch):
        per_item(ch, states)
        scan_send(0, ch, 0)

    def stage_forward(ch):
        per_item(ch, forward)
        scan_send(1, ch, 0)

    chain = (
        (stage_states, 2, 0),
        (lambda ch: scan_low(0, ch), 2, 1),
        (lambda ch: scan_top(0, ch), 2, TOP_GAP),
        (stage_forward, 3, 0),
        (lambda ch: scan_low(1, ch), 3, 1),
        (lambda ch: scan_top(1, ch), 3, TOP_GAP),
        (lambda ch: per_item(ch, backward), 3, 0),
    )
    place = [0] * n_chunks
    last_step = [0] * n_chunks
    projected = [0] * n_chunks
    cot_here = []

    def advance(p, final):
        moved = True
        while moved:
            moved = False
            for ch in range(n_chunks):
                if place[ch] == len(chain):
                    continue
                work, projs, gap = chain[place[ch]]
                if projected[ch] < projs * row_block or not (final or p >= last_step[ch] + gap):
                    continue
                if work is stage_forward and not cot_here:
                    cot_here.append(True)
                    cot_copy.wait_recv()
                    cot_local.start()
                    cot_local.wait()
                work(ch)
                place[ch] += 1
                if ch == 0 and place[ch] in (2, 5):
                    issue_to(len(pieces) - HELD_BACK[1] if place[ch] == 2 else len(pieces))
                last_step[ch] = p
                moved = True

    tok_step = (TOKEN_CUTS - 1) // 2 + 1 + len(hops)
    pending = []
    for p in range(len(pieces)):
        final = p == len(pieces) - 1
        issue_to(p + AHEAD)
        for mask in (top | pair, top, pair, 0):
            spread(mask, p)
        if final:
            pending.append(p)
        for hop in range(len(hops) + 1):
            for cut in range(TOKEN_CUTS):
                due = cut // 2 + 1 + hop
                if due == p or (final and due > p):
                    token_hop(cut, hop)
        if p >= tok_step or final:
            count = len(pending) if final else CATCH_UP
            for q in pending[:count]:
                project(q)
                projected[pieces[q][1]] += pieces[q][3]
                if final:
                    advance(p, True)
            pending = pending[count:]
            advance(p, final)
        pending.append(p)
    for copy in sends:
        copy.wait_send()


def layer(seq_count, head_parts, hidden, w_query, w_key, w_value, cotangent):
    tok_rows, width = hidden.shape
    row_block, col_width = w_query.shape
    half = col_width // 2
    heads = half // DH
    col_piece = min(half, 256)
    row_piece = row_block // ROW_CUTS
    n_chunks = half // col_piece
    chunk_heads = col_piece // DH
    n_pieces = len(cut_pieces(row_block, n_chunks))
    n_low = len(bits_below(seq_count // 4))
    anyspace = pl.BlockSpec(memory_space=pl.ANY)
    dma = pltpu.SemaphoreType.DMA
    return pl.pallas_call(
        functools.partial(layer_kernel, seq_count, head_parts),
        name="layer",
        out_shape=(
            jax.ShapeDtypeStruct((seq_count, row_block, 3 * half), BF16),
            jax.ShapeDtypeStruct((2, tok_rows, 3 * half), BF16),
        ),
        in_specs=[anyspace] * 5,
        out_specs=(anyspace, pl.BlockSpec(memory_space=pltpu.VMEM)),
        scratch_shapes=[
            pltpu.VMEM((2, tok_rows, width), BF16),
            pltpu.VMEM((row_block, 3 * half), BF16),
            pltpu.VMEM((seq_count, row_piece, col_piece), BF16),
            pltpu.VMEM((3, 2, tok_rows, half), F32),
            pltpu.VMEM((3, 2, tok_rows, half), BF16),
            pltpu.VMEM((2, heads, tok_rows, tok_rows), BF16),
            pltpu.VMEM((2, tok_rows, half), BF16),
            pltpu.VMEM((2, tok_rows, half), BF16),
            pltpu.VMEM((2, 2, heads, DH, DH), F32),
            pltpu.VMEM((2, 2, heads, DH, DH), F32),
            pltpu.VMEM((2, n_chunks, n_low, 2, chunk_heads, DH, DH), BF16),
            pltpu.VMEM((2, n_chunks, n_low, 2, chunk_heads, DH, DH), BF16),
            pltpu.VMEM((2, n_chunks, chunk_heads, DH, DH), BF16),
            pltpu.VMEM((2, n_chunks, chunk_heads, DH, DH), BF16),
            dma((seq_count, n_pieces)),
            dma((seq_count, n_pieces)),
            dma((TOKEN_CUTS, head_parts)),
            dma((TOKEN_CUTS, head_parts)),
            dma((2,)),
            dma((6,)),
            dma((seq_count,)),
            dma((2, 2, n_chunks, n_low)),
            dma((2, 2, n_chunks)),
        ],
        compiler_params=pltpu.CompilerParams(
            collective_id=0, has_side_effects=True, vmem_limit_bytes=VMEM_LIMIT
        ),
    )(hidden, w_key, w_value, w_query, cotangent)


def reduce_kernel(seq_count, head_parts, kt, lag, back, gathered, out, *scratch):
    seat = lax.axis_index("seq")
    lane = lax.axis_index("head")
    out_rows = back.shape[1]
    row_block, _ = gathered.shape[1:]
    per_block = row_block // kt
    n_tiles = seq_count * per_block
    pair = seq_count // 4
    bit = (seat // pair) % 2
    head_masks = bits_below(head_parts)
    nd = len(head_masks) + 1
    groups = 2 ** nd
    dims = [((seat, flip(lane, m)), nd - 1 - k) for k, m in enumerate(head_masks)]
    dims.append(((flip(seat, pair), lane), 0))
    orders = (
        list(range(nd)),
        [0, nd - 1] + list(range(1, nd - 1)),
    )
    rel, w_slots = scratch[0], scratch[1]
    keeps = scratch[2:2 + nd]
    send_bufs = scratch[2 + nd:2 + 2 * nd]
    recv_bufs = scratch[2 + 2 * nd:2 + 3 * nd]
    w_sem, send_sem, recv_sem = scratch[2 + 3 * nd:]

    greet([where for where, _ in dims])

    base = seat - bit * pair

    def fetch(j):
        block = xor(j // per_block, bit * pair, seq_count)
        row = pl.multiple_of((j % per_block) * kt, kt)
        return pltpu.make_async_copy(
            gathered.at[block, pl.ds(row, kt)], w_slots.at[j % 2], w_sem.at[j % 2])

    fetch(0).start()
    for g in range(groups):
        far_side = g % 2
        who = lane
        for k, m in enumerate(head_masks):
            if (g >> (nd - 1 - k)) & 1:
                who = flip(who, m)
        side = flip(bit, 1) if far_side else bit
        rel[pl.ds(g * out_rows, out_rows)] = back[side * head_parts + who]

    plans = []
    for order in orders:
        plan, current = [], list(range(groups))
        for d in order:
            place = dims[d][1]
            sent = [i for i, g in enumerate(current) if (g >> place) & 1]
            kept = [i for i, g in enumerate(current) if not (g >> place) & 1]
            plan.append((d, sent, kept))
            current = [current[i] for i in kept]
        plans.append(plan)

    def copy_of(stage, tile, where):
        return pltpu.make_async_remote_copy(
            src_ref=send_bufs[stage].at[tile], dst_ref=recv_bufs[stage].at[tile],
            send_sem=send_sem.at[stage, tile], recv_sem=recv_sem.at[stage, tile],
            device_id=where, device_id_type=MESH)

    rows_half = groups // 2 * out_rows

    def multiply(j, plan):
        fetch(j).wait()

        @pl.when(j + 1 < n_tiles)
        def _():
            fetch(j + 1).start()

        w = w_slots[j % 2]
        contract = (((1,), (1,)), ((), ()))
        away = lax.dot_general(rel[pl.ds(rows_half, rows_half)], w, contract,
                               preferred_element_type=F32)
        send_bufs[0][j] = away.astype(BF16).reshape(groups // 2, out_rows, kt)
        copy_of(0, j, dims[plan[0][0]][0]).start()
        home = lax.dot_general(rel[pl.ds(0, rows_half)], w, contract, preferred_element_type=F32)
        keeps[0][j % keeps[0].shape[0]] = home.reshape(groups // 2, out_rows, kt)

    def forward(stage, j, plan):
        copy_of(stage - 1, j, dims[plan[stage - 1][0]][0]).wait_recv()
        slot = j % keeps[stage - 1].shape[0]
        if stage == nd:
            total = keeps[stage - 1][slot, 0] + recv_bufs[stage - 1][j, 0].astype(F32)
            block = xor(base, j // per_block, seq_count)
            column = pl.multiple_of(block * row_block + (j % per_block) * kt, kt)
            out[:, pl.ds(column, kt)] = total
            return
        d, sent, kept = plan[stage]
        for k, i in enumerate(sent):
            total = keeps[stage - 1][slot, i] + recv_bufs[stage - 1][j, i].astype(F32)
            send_bufs[stage][j, k] = total.astype(BF16)
        copy_of(stage, j, dims[d][0]).start()
        here = j % keeps[stage].shape[0]
        for k, i in enumerate(kept):
            keeps[stage][here, k] = keeps[stage - 1][slot, i] + recv_bufs[stage - 1][j, i].astype(F32)

    delays = [0] + [1 + lag * s for s in range(nd)]
    steps = n_tiles + delays[-1]

    def step(i, carry):
        for parity in range(2):
            now = i * 2 + parity

            @pl.when(now < n_tiles)
            def _():
                multiply(now, plans[parity])

            for stage in range(1, nd + 1):
                j = now - delays[stage]
                plan = plans[(parity - delays[stage]) % 2]

                @pl.when((j >= 0) & (j < n_tiles))
                def _():
                    forward(stage, j, plan)
        return carry

    lax.fori_loop(0, (steps + 1) // 2, step, 0)

    def drain(j, carry):
        for stage in range(nd):
            copy_of(stage, j, dims[0][0]).wait_send()
        return carry

    lax.fori_loop(0, n_tiles, drain, 0)


def project_back(seq_count, head_parts, back, gathered):
    groups, out_rows, depth = back.shape
    row_block = gathered.shape[1]
    kt = row_block // 2
    n_tiles = seq_count * 2
    lag = 3
    nd = len(bits_below(head_parts)) + 1
    sizes = [groups >> (s + 1) for s in range(nd)]
    return pl.pallas_call(
        functools.partial(reduce_kernel, seq_count, head_parts, kt, lag),
        name="project_back",
        out_shape=jax.ShapeDtypeStruct((out_rows, seq_count * row_block), F32),
        in_specs=[pl.BlockSpec(memory_space=pltpu.VMEM), pl.BlockSpec(memory_space=pl.ANY)],
        out_specs=pl.BlockSpec(memory_space=pltpu.VMEM),
        scratch_shapes=[
            pltpu.VMEM((groups * out_rows, depth), BF16),
            pltpu.VMEM((2, kt, depth), BF16),
            *[pltpu.VMEM((2 if s == 0 else lag + 1, n, out_rows, kt), F32)
              for s, n in enumerate(sizes)],
            *[pltpu.VMEM((n_tiles, n, out_rows, kt), BF16) for n in sizes],
            *[pltpu.VMEM((n_tiles, n, out_rows, kt), BF16) for n in sizes],
            pltpu.SemaphoreType.DMA((2,)),
            pltpu.SemaphoreType.DMA((nd, n_tiles)),
            pltpu.SemaphoreType.DMA((nd, n_tiles)),
        ],
        compiler_params=pltpu.CompilerParams(
            collective_id=1, has_side_effects=True, vmem_limit_bytes=VMEM_LIMIT
        ),
    )(back, gathered)


def on_device(seq_count, head_parts, hidden, w_query, w_key, w_value, cotangent):
    gathered, back = layer(seq_count, head_parts, hidden, w_query, w_key, w_value, cotangent)
    groups = 2 * head_parts
    back = back.reshape(groups, hidden.shape[0] // head_parts, back.shape[2])
    input_grad = project_back(seq_count, head_parts, back, gathered)
    factor = lax.rsqrt(jnp.mean(input_grad * input_grad, axis=-1, keepdims=True) + STEP_EPS)
    return jnp.tanh(input_grad * factor)


def solution(mesh):
    def body(*args):
        return on_device(mesh.shape["seq"], mesh.shape["head"], *args)

    return jax.shard_map(
        body,
        mesh=mesh,
        in_specs=(
            P("seq", None),
            P("seq", "head"),
            P("seq", "head"),
            P("seq", "head"),
            P("seq", "head"),
        ),
        out_specs=P(("seq", "head"), None),
        check_vma=False,
    )
```

time: 532 us -> 421 us (0.79)
  local copies, waits for them, and re-layouts: 30.7 us -> 0.74 us
  Pallas kernels: 444 us -> 415 us
  matrix products: 28.4 us -> 0 us
  other arithmetic: 19.6 us -> 5.33 us
    pallas_call x1, Pallas kernels: 361 us -> 329 us  [layer(): pl.pallas_call(functools.partial(layer_kernel, seq_count, head_parts), na...]
    dot_general x12 -> x0, matrix products: 28.4 us -> none  [the longest x1 4.31 us: attend(): jnp.einsum('bthj,bhij->bthi', value_rows.astype(F32), later_sum, precisio...]
    convert_element_type x4 -> x0, local copies, waits for them, and re-layouts: 7.42 us -> none  [the longest x1 2.54 us: attend(): back_value = grad_value.astype(BF16)]
    convert_element_type x4 -> x0, other arithmetic: 7.21 us -> none  [the longest x2 3.4 us: scan_states(): other = swap(whole.astype(BF16), 'seq', top, seq_count).astype(F32)]
    slice x2 -> x0, local copies, waits for them, and re-layouts: 6.9 us -> none  [attend(): pre_key, pre_value, pre_query = (pre[i].reshape(shape) for i in range(3))]
    another operation x3 -> x0, local copies, waits for them, and re-layouts: 6.85 us -> none  [the longest x2 4.77 us: attend(): pre_key, pre_value, pre_query = (pre[i].reshape(shape) for i in range(3))]
  transfers between devices with their start and end apart: 4 -> 0, of which waited for: 1 -> 0; matrix products, arithmetic and copies ran while one was open for 4% -> 0% of each run, Pallas kernels for 0% -> 0%
where the time goes in v1:
time: 421 us
  Pallas kernels  415 us (99%)
  other arithmetic  5.33 us (1%)
    pallas_call x1, Pallas kernels, layer(): pl.pallas_call(functools.partial(layer_kernel, seq_count, head_parts), na...  329 us
    pallas_call x1, Pallas kernels, project_back(): pl.pallas_call(functools.partial(reduce_kernel, seq_count, head_parts, kt...  85.9 us

profile of v1, /device:TPU:0, one launch (start us, length us, event | category | flops | bytes accessed | tf_op | source)
XLA Modules:
  0.0 420.7 jit_solution(17880653189911322661)
XLA Ops:
  0.0 328.6 %layer.1 = (bf16[8,1024,1536]{2,1,0:T(8,128)(2,1)}, bf16[2,512,1536]{2,1,0:T(8,128)(2,1)}) custom-call(bf16[512,8192]{1,0:T(8,128)(2,1)} %hidden.1, bf16[1024,1024]{1,0:T(8,128)(2,1)} %w_key.1, bf16[1024,1024]{1,0:T(8,128)(2,1)} %w_value.1, bf16[1024,1024]{1,0:T(8,128)(2,1)} %w_query.1, bf16[512,1024]{1,0:T(8,128)(2,1)} %cot.1), custom_call_target="tpu_custom_call" | custom-call | tf_op jit(solution)/shard_map/layer/pallas_call | solution.py:443
  328.6 85.9 %project_back.1 = f32[128,8192]{1,0:T(8,128)} custom-call(bf16[8,128,1536]{2,1,0:T(8,128)(2,1)} %bitcast.1, bf16[8,1024,1536]{2,1,0:T(8,128)(2,1)} %get-tuple-element.8.gathered), custom_call_target="tpu_custom_call" | custom-call | tf_op jit(solution)/shard_map/project_back/pallas_call | solution.py:618
  414.6 0.0 copy-start
  414.6 2.7 multiply_reduce_fusion
  417.3 0.7 copy-done
  418.0 2.6 multiply_tanh_fusion
  (1 shorter events, 0.0 us)
Async XLA Ops:
  414.6 3.5 copy-start

commit v2 on v1

--- a/solution.py
+++ b/solution.py
@@ -20,9 +20,12 @@
 LAST_CUTS = (2, 1, 1)
 AHEAD = 2
 HELD_BACK = (2, 2)
-TOP_GAP = 4
+TOP_GAPS = (4, 13)
 TOKEN_CUTS = 4
-CATCH_UP = 4
+CATCH_UP = 2
+UNROLL = 1
+TILE_CUTS = 2
+LAG = 3
 
 
 def silu_slope(preact):
@@ -76,7 +79,7 @@
 
 
 def layer_kernel(seq_count, head_parts, hidden, w_key, w_value, w_query, cot,
-                 gathered, back, tokens, own, stage, pre, act, scores, grads, cot_rows,
+                 gathered, back, tokens, own, stage, pre, act, partial, grads, cot_rows,
                  outside, total, low_send, low_recv, top_send, top_recv,
                  w_send, w_recv, tok_send, tok_recv, cot_sems, local, fetch,
                  low_sems, top_sems):
@@ -252,18 +255,15 @@
         lax.fori_loop(0, seq_count, block_dot, 0)
 
 
-    def per_item(ch, work):
+    def per_item(ch, work, first=0, past=2 * chunk_heads):
         def item(i, carry):
             head = ch * chunk_heads + i % chunk_heads
             work(i // chunk_heads, head, pl.ds(pl.multiple_of(head * DH, DH), DH))
             return carry
 
-        lax.fori_loop(0, 2 * chunk_heads, item, 0)
-
-    causal = (
-        lax.broadcasted_iota(jnp.int32, (tok_rows, tok_rows), 0)
-        >= lax.broadcasted_iota(jnp.int32, (tok_rows, tok_rows), 1)
-    )
+        lax.fori_loop(first, past, item, 0, unroll=UNROLL)
+
+    band = tok_rows // 2
 
     def dot(left, right, left_dim, right_dim):
         return lax.dot_general(left, right, (((left_dim,), (right_dim,)), ((), ())),
@@ -280,36 +280,61 @@
     def forward(side, head, cols):
         query = jax.nn.silu(pre[2, side, :, cols]).astype(BF16)
         act[2, side, :, cols] = query
-        key, value = act[0, side, :, cols], act[1, side, :, cols]
-        masked = jnp.where(causal, dot(query, key, 1, 1), 0.0).astype(BF16)
-        scores[side, head] = masked
-        attended = dot(masked, value, 1, 0) + dot(query, outside[0, side, head].astype(BF16), 1, 0)
-        scale = lax.rsqrt(jnp.mean(attended * attended, axis=-1, keepdims=True) + NORM_EPS)
-        normed = attended * scale
-        upstream = cot_rows[side, :, cols].astype(F32)
-        grad = scale * (upstream - normed * jnp.mean(upstream * normed, axis=-1, keepdims=True))
-        grad = grad.astype(BF16)
-        grads[side, :, cols] = grad
-        total[1, side, head] = dot(query, grad, 0, 0)
+        before = outside[0, side, head].astype(BF16)
+        own_grad = jnp.zeros((DH, DH), F32)
+        for start_row in (0, band):
+            rows, past = pl.ds(start_row, band), start_row + band
+            near_query = query[start_row:past]
+            key, value = act[0, side, pl.ds(0, past), cols], act[1, side, pl.ds(0, past), cols]
+            row = lax.broadcasted_iota(jnp.int32, (band, past), 0) + start_row
+            column = lax.broadcasted_iota(jnp.int32, (band, past), 1)
+            scores = jnp.where(row >= column, dot(near_query, key, 1, 1), 0.0).astype(BF16)
+            attended = dot(scores, value, 1, 0) + dot(near_query, before, 1, 0)
+            scale = lax.rsqrt(jnp.mean(attended * attended, axis=-1, keepdims=True) + NORM_EPS)
+            normed = attended * scale
+            upstream = cot_rows[side, rows, cols].astype(F32)
+            grad = scale * (
+                upstream - normed * jnp.mean(upstream * normed, axis=-1, keepdims=True))
+            grad = grad.astype(BF16)
+            grads[side, rows, cols] = grad
+            own_grad += dot(near_query, grad, 0, 0)
+        total[1, side, head] = own_grad
         outside[1, side, head] = jnp.zeros((DH, DH), F32)
 
-    def backward(side, head, cols):
+    def to_back(proj, side, head, rows, result):
+        column = pl.ds(pl.multiple_of(proj * half + head * DH, DH), DH)
+        back[side, rows, column] = result.astype(BF16)
+
+    def inner(side, head, cols):
         key, value, query = (act[i, side, :, cols] for i in range(3))
         grad = grads[side, :, cols]
         before = outside[0, side, head].astype(BF16)
+        for start_row in (0, band):
+            rows, past = pl.ds(start_row, band), start_row + band
+            row = lax.broadcasted_iota(jnp.int32, (band, past), 0) + start_row
+            column = lax.broadcasted_iota(jnp.int32, (band, past), 1)
+            near = grad[start_row:past]
+            grad_scores = jnp.where(row >= column, dot(near, value[:past], 1, 1), 0.0).astype(BF16)
+            grad_query = dot(grad_scores, key[:past], 1, 0) + dot(near, before, 1, 1)
+            to_back(2, side, head, rows, grad_query * silu_slope(pre[2, side, rows, cols]))
+            key_row = lax.broadcasted_iota(jnp.int32, (band, tok_rows - start_row), 0)
+            token = lax.broadcasted_iota(jnp.int32, (band, tok_rows - start_row), 1)
+            turned = jnp.where(
+                key_row <= token, dot(value[start_row:past], grad[start_row:], 1, 1), 0.0
+            ).astype(BF16)
+            partial[side, rows, cols] = dot(turned, query[start_row:], 1, 0)
+            turned = jnp.where(
+                key_row <= token, dot(key[start_row:past], query[start_row:], 1, 1), 0.0
+            ).astype(BF16)
+            pre[1, side, rows, cols] = dot(turned, grad[start_row:], 1, 0)
+
+    def finish(side, head, cols):
         after = outside[1, side, head].astype(BF16)
-        grad_scores = jnp.where(causal, dot(grad, value, 1, 1), 0.0).astype(BF16)
-        grad_query = dot(grad_scores, key, 1, 0) + dot(grad, before, 1, 1)
-        grad_key = dot(grad_scores, query, 0, 0) + dot(value, after, 1, 1)
-        grad_value = dot(scores[side, head], grad, 0, 0) + dot(key, after, 1, 0)
-        results = (
-            grad_key * silu_slope(pre[0, side, :, cols]),
-            grad_value,
-            grad_query * silu_slope(pre[2, side, :, cols]),
-        )
-        for proj, result in enumerate(results):
-            column = pl.ds(pl.multiple_of(proj * half + head * DH, DH), DH)
-            back[side, :, column] = result.astype(BF16)
+        grad_key = partial[side, :, cols] + dot(act[1, side, :, cols], after, 1, 1)
+        grad_value = pre[1, side, :, cols] + dot(act[0, side, :, cols], after, 1, 0)
+        rows = pl.ds(0, tok_rows)
+        to_back(0, side, head, rows, grad_key * silu_slope(pre[0, side, :, cols]))
+        to_back(1, side, head, rows, grad_value)
 
 
     def heads_of(ch):
@@ -366,11 +391,13 @@
     chain = (
         (stage_states, 2, 0),
         (lambda ch: scan_low(0, ch), 2, 1),
-        (lambda ch: scan_top(0, ch), 2, TOP_GAP),
+        (lambda ch: scan_top(0, ch), 2, TOP_GAPS[0]),
         (stage_forward, 3, 0),
-        (lambda ch: scan_low(1, ch), 3, 1),
-        (lambda ch: scan_top(1, ch), 3, TOP_GAP),
-        (lambda ch: per_item(ch, backward), 3, 0),
+        (lambda ch: per_item(ch, inner, 0, chunk_heads), 3, 0),
+        (lambda ch: scan_low(1, ch), 3, 0),
+        (lambda ch: per_item(ch, inner, chunk_heads), 3, 1),
+        (lambda ch: scan_top(1, ch), 3, TOP_GAPS[1]),
+        (lambda ch: per_item(ch, finish), 3, 0),
     )
     place = [0] * n_chunks
     last_step = [0] * n_chunks
@@ -394,7 +421,7 @@
                     cot_local.wait()
                 work(ch)
                 place[ch] += 1
-                if ch == 0 and place[ch] in (2, 5):
+                if ch == 0 and place[ch] in (2, 6):
                     issue_to(len(pieces) - HELD_BACK[1] if place[ch] == 2 else len(pieces))
                 last_step[ch] = p
                 moved = True
@@ -455,7 +482,7 @@
             pltpu.VMEM((seq_count, row_piece, col_piece), BF16),
             pltpu.VMEM((3, 2, tok_rows, half), F32),
             pltpu.VMEM((3, 2, tok_rows, half), BF16),
-            pltpu.VMEM((2, heads, tok_rows, tok_rows), BF16),
+            pltpu.VMEM((2, tok_rows, half), F32),
             pltpu.VMEM((2, tok_rows, half), BF16),
             pltpu.VMEM((2, tok_rows, half), BF16),
             pltpu.VMEM((2, 2, heads, DH, DH), F32),
@@ -480,7 +507,7 @@
     )(hidden, w_key, w_value, w_query, cotangent)
 
 
-def reduce_kernel(seq_count, head_parts, kt, lag, back, gathered, out, *scratch):
+def reduce_kernel(seq_count, head_parts, kt, lag, back, gathered, out, factor, *scratch):
     seat = lax.axis_index("seq")
     lane = lax.axis_index("head")
     out_rows = back.shape[1]
@@ -502,7 +529,7 @@
     keeps = scratch[2:2 + nd]
     send_bufs = scratch[2 + nd:2 + 2 * nd]
     recv_bufs = scratch[2 + 2 * nd:2 + 3 * nd]
-    w_sem, send_sem, recv_sem = scratch[2 + 3 * nd:]
+    squares, w_sem, send_sem, recv_sem = scratch[2 + 3 * nd:]
 
     greet([where for where, _ in dims])
 
@@ -515,6 +542,7 @@
             gathered.at[block, pl.ds(row, kt)], w_slots.at[j % 2], w_sem.at[j % 2])
 
     fetch(0).start()
+    squares[...] = jnp.zeros_like(squares)
     for g in range(groups):
         far_side = g % 2
         who = lane
@@ -567,6 +595,8 @@
             block = xor(base, j // per_block, seq_count)
             column = pl.multiple_of(block * row_block + (j % per_block) * kt, kt)
             out[:, pl.ds(column, kt)] = total
+            for k in range(kt // DH):
+                squares[...] += total[:, k * DH:(k + 1) * DH] * total[:, k * DH:(k + 1) * DH]
             return
         d, sent, kept = plan[stage]
         for k, i in enumerate(sent):
@@ -599,6 +629,9 @@
 
     lax.fori_loop(0, (steps + 1) // 2, step, 0)
 
+    mean = jnp.sum(squares[...], axis=-1, keepdims=True) / out.shape[1]
+    factor[...] = jnp.broadcast_to(lax.rsqrt(mean + STEP_EPS), factor.shape)
+
     def drain(j, carry):
         for stage in range(nd):
             copy_of(stage, j, dims[0][0]).wait_send()
@@ -610,17 +643,20 @@
 def project_back(seq_count, head_parts, back, gathered):
     groups, out_rows, depth = back.shape
     row_block = gathered.shape[1]
-    kt = row_block // 2
-    n_tiles = seq_count * 2
-    lag = 3
+    kt = row_block // TILE_CUTS
+    n_tiles = seq_count * TILE_CUTS
+    lag = LAG
     nd = len(bits_below(head_parts)) + 1
     sizes = [groups >> (s + 1) for s in range(nd)]
     return pl.pallas_call(
         functools.partial(reduce_kernel, seq_count, head_parts, kt, lag),
         name="project_back",
-        out_shape=jax.ShapeDtypeStruct((out_rows, seq_count * row_block), F32),
+        out_shape=(
+            jax.ShapeDtypeStruct((out_rows, seq_count * row_block), F32),
+            jax.ShapeDtypeStruct((out_rows, DH), F32),
+        ),
         in_specs=[pl.BlockSpec(memory_space=pltpu.VMEM), pl.BlockSpec(memory_space=pl.ANY)],
-        out_specs=pl.BlockSpec(memory_space=pltpu.VMEM),
+        out_specs=(pl.BlockSpec(memory_space=pltpu.VMEM),) * 2,
         scratch_shapes=[
             pltpu.VMEM((groups * out_rows, depth), BF16),
             pltpu.VMEM((2, kt, depth), BF16),
@@ -628,6 +664,7 @@
               for s, n in enumerate(sizes)],
             *[pltpu.VMEM((n_tiles, n, out_rows, kt), BF16) for n in sizes],
             *[pltpu.VMEM((n_tiles, n, out_rows, kt), BF16) for n in sizes],
+            pltpu.VMEM((out_rows, DH), F32),
             pltpu.SemaphoreType.DMA((2,)),
             pltpu.SemaphoreType.DMA((nd, n_tiles)),
             pltpu.SemaphoreType.DMA((nd, n_tiles)),
@@ -642,9 +679,8 @@
     gathered, back = layer(seq_count, head_parts, hidden, w_query, w_key, w_value, cotangent)
     groups = 2 * head_parts
     back = back.reshape(groups, hidden.shape[0] // head_parts, back.shape[2])
-    input_grad = project_back(seq_count, head_parts, back, gathered)
-    factor = lax.rsqrt(jnp.mean(input_grad * input_grad, axis=-1, keepdims=True) + STEP_EPS)
-    return jnp.tanh(input_grad * factor)
+    input_grad, factor = project_back(seq_count, head_parts, back, gathered)
+    return jnp.tanh(input_grad * factor[:, :1])
 
 
 def solution(mesh):

time: 421 us -> 418 us (level)
  no operation moved by 1% of the time
where the time goes in v2:
time: 418 us
  Pallas kernels  412 us (99%)
  other arithmetic  4.82 us (1%)
    pallas_call x1, Pallas kernels, layer(): pl.pallas_call(functools.partial(layer_kernel, seq_count, head_parts), na...  330 us
    pallas_call x1, Pallas kernels, project_back(): pl.pallas_call(functools.partial(reduce_kernel, seq_count, head_parts, kt...  82.2 us

profile of v2, /device:TPU:0, one launch (start us, length us, event | category | flops | bytes accessed | tf_op | source)
XLA Modules:
  0.0 417.8 jit_solution(9227297643184888568)
XLA Ops:
  0.0 329.8 %layer.1 = (bf16[8,1024,1536]{2,1,0:T(8,128)(2,1)}, bf16[2,512,1536]{2,1,0:T(8,128)(2,1)}) custom-call(bf16[512,8192]{1,0:T(8,128)(2,1)} %hidden.1, bf16[1024,1024]{1,0:T(8,128)(2,1)} %w_key.1, bf16[1024,1024]{1,0:T(8,128)(2,1)} %w_value.1, bf16[1024,1024]{1,0:T(8,128)(2,1)} %w_query.1, bf16[512,1024]{1,0:T(8,128)(2,1)} %cot.1), custom_call_target="tpu_custom_call" | custom-call | tf_op jit(solution)/shard_map/layer/pallas_call | solution.py:470
  329.9 82.2 %project_back.1 = (f32[128,8192]{1,0:T(8,128)}, f32[128,128]{1,0:T(8,128)}) custom-call(bf16[8,128,1536]{2,1,0:T(8,128)(2,1)} %bitcast.1, bf16[8,1024,1536]{2,1,0:T(8,128)(2,1)} %get-tuple-element.10.gathered), custom_call_target="tpu_custom_call" | custom-call | tf_op jit(solution)/shard_map/project_back/pallas_call | solution.py:651
  412.0 0.9 slice_reduce_fusion
  413.0 4.8 %multiply_tanh_fusion = f32[128,8192]{1,0:T(8,128)} fusion(f32[128,8192]{1,0:T(8,128)} %get-tuple-element.11, f32[128]{0:T(128)S(1)} %slice_reduce_fusion), kind=kLoop, calls=%fused_computation | loop fusion | flops 1048576 | bytes 8389120 | tf_op jit(solution)/shard_map/tanh | solution.py:683

commit v3 on v2

--- a/solution.py
+++ b/solution.py
@@ -26,6 +26,7 @@
 UNROLL = 1
 TILE_CUTS = 2
 LAG = 3
+OUT_SLOTS = 4
 
 
 def silu_slope(preact):
@@ -79,10 +80,10 @@
 
 
 def layer_kernel(seq_count, head_parts, hidden, w_key, w_value, w_query, cot,
-                 gathered, back, tokens, own, stage, pre, act, partial, grads, cot_rows,
-                 outside, total, low_send, low_recv, top_send, top_recv,
+                 gathered, back_out, tokens, own, stage, pre, act, partial, grads, cot_rows,
+                 outside, total, low_send, low_recv, top_send, top_recv, back,
                  w_send, w_recv, tok_send, tok_recv, cot_sems, local, fetch,
-                 low_sems, top_sems):
+                 low_sems, top_sems, back_sems):
     seat = lax.axis_index("seq")
     lane = lax.axis_index("head")
     tok_rows, _ = hidden.shape
@@ -388,6 +389,17 @@
         per_item(ch, forward)
         scan_send(1, ch, 0)
 
+    back_copies = []
+
+    def stage_finish(ch):
+        per_item(ch, finish)
+        for proj in range(3):
+            columns = pl.ds(proj * half + ch * col_piece, col_piece)
+            copy = pltpu.make_async_copy(
+                back.at[:, :, columns], back_out.at[:, :, columns], back_sems.at[proj, ch])
+            copy.start()
+            back_copies.append(copy)
+
     chain = (
         (stage_states, 2, 0),
         (lambda ch: scan_low(0, ch), 2, 1),
@@ -397,7 +409,7 @@
         (lambda ch: scan_low(1, ch), 3, 0),
         (lambda ch: per_item(ch, inner, chunk_heads), 3, 1),
         (lambda ch: scan_top(1, ch), 3, TOP_GAPS[1]),
-        (lambda ch: per_item(ch, finish), 3, 0),
+        (stage_finish, 3, 0),
     )
     place = [0] * n_chunks
     last_step = [0] * n_chunks
@@ -452,6 +464,8 @@
         pending.append(p)
     for copy in sends:
         copy.wait_send()
+    for copy in back_copies:
+        copy.wait()
 
 
 def layer(seq_count, head_parts, hidden, w_query, w_key, w_value, cotangent):
@@ -475,7 +489,7 @@
             jax.ShapeDtypeStruct((2, tok_rows, 3 * half), BF16),
         ),
         in_specs=[anyspace] * 5,
-        out_specs=(anyspace, pl.BlockSpec(memory_space=pltpu.VMEM)),
+        out_specs=(anyspace, anyspace),
         scratch_shapes=[
             pltpu.VMEM((2, tok_rows, width), BF16),
             pltpu.VMEM((row_block, 3 * half), BF16),
@@ -491,6 +505,7 @@
             pltpu.VMEM((2, n_chunks, n_low, 2, chunk_heads, DH, DH), BF16),
             pltpu.VMEM((2, n_chunks, chunk_heads, DH, DH), BF16),
             pltpu.VMEM((2, n_chunks, chunk_heads, DH, DH), BF16),
+            pltpu.VMEM((2, tok_rows, 3 * half), BF16),
             dma((seq_count, n_pieces)),
             dma((seq_count, n_pieces)),
             dma((TOKEN_CUTS, head_parts)),
@@ -500,6 +515,7 @@
             dma((seq_count,)),
             dma((2, 2, n_chunks, n_low)),
             dma((2, 2, n_chunks)),
+            dma((3, n_chunks)),
         ],
         compiler_params=pltpu.CompilerParams(
             collective_id=0, has_side_effects=True, vmem_limit_bytes=VMEM_LIMIT
@@ -529,9 +545,7 @@
     keeps = scratch[2:2 + nd]
     send_bufs = scratch[2 + nd:2 + 2 * nd]
     recv_bufs = scratch[2 + 2 * nd:2 + 3 * nd]
-    squares, w_sem, send_sem, recv_sem = scratch[2 + 3 * nd:]
-
-    greet([where for where, _ in dims])
+    squares, out_slots, w_sem, rel_sem, out_sem, send_sem, recv_sem = scratch[2 + 3 * nd:]
 
     base = seat - bit * pair
 
@@ -543,6 +557,7 @@
 
     fetch(0).start()
     squares[...] = jnp.zeros_like(squares)
+    rel_copies = []
     for g in range(groups):
         far_side = g % 2
         who = lane
@@ -550,7 +565,13 @@
             if (g >> (nd - 1 - k)) & 1:
                 who = flip(who, m)
         side = flip(bit, 1) if far_side else bit
-        rel[pl.ds(g * out_rows, out_rows)] = back[side * head_parts + who]
+        copy = pltpu.make_async_copy(
+            back.at[side * head_parts + who], rel.at[pl.ds(g * out_rows, out_rows)], rel_sem.at[g])
+        copy.start()
+        rel_copies.append(copy)
+    greet([where for where, _ in dims])
+    for copy in rel_copies:
+        copy.wait()
 
     plans = []
     for order in orders:
@@ -569,6 +590,12 @@
             send_sem=send_sem.at[stage, tile], recv_sem=recv_sem.at[stage, tile],
             device_id=where, device_id_type=MESH)
 
+    def copy_out(j):
+        block = xor(base, j // per_block, seq_count)
+        column = pl.multiple_of(block * row_block + (j % per_block) * kt, kt)
+        return pltpu.make_async_copy(
+            out_slots.at[j % OUT_SLOTS], out.at[:, pl.ds(column, kt)], out_sem.at[j % OUT_SLOTS])
+
     rows_half = groups // 2 * out_rows
 
     def multiply(j, plan):
@@ -592,9 +619,13 @@
         slot = j % keeps[stage - 1].shape[0]
         if stage == nd:
             total = keeps[stage - 1][slot, 0] + recv_bufs[stage - 1][j, 0].astype(F32)
-            block = xor(base, j // per_block, seq_count)
-            column = pl.multiple_of(block * row_block + (j % per_block) * kt, kt)
-            out[:, pl.ds(column, kt)] = total
+
+            @pl.when(j >= OUT_SLOTS)
+            def _():
+                copy_out(j - OUT_SLOTS).wait()
+
+            out_slots[j % OUT_SLOTS] = total
+            copy_out(j).start()
             for k in range(kt // DH):
                 squares[...] += total[:, k * DH:(k + 1) * DH] * total[:, k * DH:(k + 1) * DH]
             return
@@ -638,6 +669,8 @@
         return carry
 
     lax.fori_loop(0, n_tiles, drain, 0)
+    for j in range(n_tiles - OUT_SLOTS, n_tiles):
+        copy_out(j).wait()
 
 
 def project_back(seq_count, head_parts, back, gathered):
@@ -655,8 +688,10 @@
             jax.ShapeDtypeStruct((out_rows, seq_count * row_block), F32),
             jax.ShapeDtypeStruct((out_rows, DH), F32),
         ),
-        in_specs=[pl.BlockSpec(memory_space=pltpu.VMEM), pl.BlockSpec(memory_space=pl.ANY)],
-        out_specs=(pl.BlockSpec(memory_space=pltpu.VMEM),) * 2,
+        in_specs=[pl.BlockSpec(memory_space=pl.ANY)] * 2,
+        out_specs=(
+            pl.BlockSpec(memory_space=pl.ANY), pl.BlockSpec(memory_space=pltpu.VMEM),
+        ),
         scratch_shapes=[
             pltpu.VMEM((groups * out_rows, depth), BF16),
             pltpu.VMEM((2, kt, depth), BF16),
@@ -665,7 +700,10 @@
             *[pltpu.VMEM((n_tiles, n, out_rows, kt), BF16) for n in sizes],
             *[pltpu.VMEM((n_tiles, n, out_rows, kt), BF16) for n in sizes],
             pltpu.VMEM((out_rows, DH), F32),
+            pltpu.VMEM((OUT_SLOTS, out_rows, kt), F32),
             pltpu.SemaphoreType.DMA((2,)),
+            pltpu.SemaphoreType.DMA((groups,)),
+            pltpu.SemaphoreType.DMA((OUT_SLOTS,)),
             pltpu.SemaphoreType.DMA((nd, n_tiles)),
             pltpu.SemaphoreType.DMA((nd, n_tiles)),
         ],

time: 418 us -> 414 us (level)
  no operation moved by 1% of the time
where the time goes in v3:
time: 414 us
  Pallas kernels  408 us (99%)
  other arithmetic  4.82 us (1%)
    pallas_call x1, Pallas kernels, layer(): pl.pallas_call(functools.partial(layer_kernel, seq_count, head_parts), na...  330 us
    pallas_call x1, Pallas kernels, project_back(): pl.pallas_call(functools.partial(reduce_kernel, seq_count, head_parts, kt...  78.3 us

profile of v3, /device:TPU:0, one launch (start us, length us, event | category | flops | bytes accessed | tf_op | source)
XLA Modules:
  0.0 413.8 jit_solution(13501064936801243246)
XLA Ops:
  0.0 329.8 %layer.1 = (bf16[8,1024,1536]{2,1,0:T(8,128)(2,1)}, bf16[2,512,1536]{2,1,0:T(8,128)(2,1)}) custom-call(bf16[512,8192]{1,0:T(8,128)(2,1)} %hidden.1, bf16[1024,1024]{1,0:T(8,128)(2,1)} %w_key.1, bf16[1024,1024]{1,0:T(8,128)(2,1)} %w_value.1, bf16[1024,1024]{1,0:T(8,128)(2,1)} %w_query.1, bf16[512,1024]{1,0:T(8,128)(2,1)} %cot.1), custom_call_target="tpu_custom_call" | custom-call | tf_op jit(solution)/shard_map/layer/pallas_call | solution.py:484
  329.8 78.3 %project_back.1 = (f32[128,8192]{1,0:T(8,128)}, f32[128,128]{1,0:T(8,128)}) custom-call(bf16[8,128,1536]{2,1,0:T(8,128)(2,1)} %bitcast.1, bf16[8,1024,1536]{2,1,0:T(8,128)(2,1)} %get-tuple-element.10.gathered), custom_call_target="tpu_custom_call" | custom-call | tf_op jit(solution)/shard_map/project_back/pallas_call | solution.py:684
  408.1 0.9 slice_reduce_fusion
  409.0 4.8 %multiply_tanh_fusion = f32[128,8192]{1,0:T(8,128)} fusion(f32[128,8192]{1,0:T(8,128)} %get-tuple-element.11, f32[128]{0:T(128)S(1)} %slice_reduce_fusion), kind=kLoop, calls=%fused_computation | loop fusion | flops 1048576 | bytes 8389120 | tf_op jit(solution)/shard_map/tanh | solution.py:721
